TPU v7x, 32 devices: a whole 2x2x4 slice. The times are simulated.
32 devices in a mesh: dp: 16 (over z, y, x), mp: 2 (over core).
Axes of the slice: x: 2, y: 2, z: 4, core: 2. Of those that a mesh axis runs over, the one named last changes fastest.
Arguments:
- tokens: bfloat16 [16384, 768], P('dp'), may hold values from -6 to 6
- cotangent: bfloat16 [16384, 768], P('dp'), may hold values from -6 to 6
- seg_lengths: int32 [32, 8], P('dp'), may hold values from 1 to 256, 512 in all within a row
- pad_counts: int32 [32], P('dp'), may hold values from 0 to 64
- qkv_weight: float32 [3, 768, 768], P(None, 'dp', 'mp'), may hold values from -0.3125 to 0.3125
- first_qkv: float32 [3, 768, 768], P(None, 'dp', 'mp'), may hold values from -0.00024414062 to 0.00024414062
- second_qkv: float32 [3, 768, 768], P(None, 'dp', 'mp'), may hold values from 7.4315953e-09 to 2.974051e-08
- average_qkv: float32 [3, 768, 768], P(None, 'dp', 'mp'), may hold values from -0.3125 to 0.3125
- attn_weight: float32 [768, 768], P(('mp', 'dp')), may hold values from -0.625 to 0.625
- first_attn: float32 [768, 768], P(('mp', 'dp')), may hold values from -0.00024414062 to 0.00024414062
- second_attn: float32 [768, 768], P(('mp', 'dp')), may hold values from 7.4315953e-09 to 2.974051e-08
- average_attn: float32 [768, 768], P(('mp', 'dp')), may hold values from -0.625 to 0.625
- up_weight: float32 [768, 3072], P('dp', 'mp'), may hold values from -0.21875 to 0.21875
- first_up: float32 [768, 3072], P('dp', 'mp'), may hold values from -0.00024414062 to 0.00024414062
- second_up: float32 [768, 3072], P('dp', 'mp'), may hold values from 7.4315953e-09 to 2.974051e-08
- average_up: float32 [768, 3072], P('dp', 'mp'), may hold values from -0.21875 to 0.21875
- down_weight: float32 [3072, 768], P(('mp', 'dp')), may hold values from -0.109375 to 0.109375
- first_down: float32 [3072, 768], P(('mp', 'dp')), may hold values from -0.00024414062 to 0.00024414062
- second_down: float32 [3072, 768], P(('mp', 'dp')), may hold values from 7.4315953e-09 to 2.974051e-08
- average_down: float32 [3072, 768], P(('mp', 'dp')), may hold values from -0.109375 to 0.109375
- head_bias: float32 [2, 768], P(None, ('mp', 'dp')), may hold values from -1.75 to 1.75
- first_head: float32 [2, 768], P(None, ('mp', 'dp')), may hold values from -0.00048828125 to 0.00048828125
- second_head: float32 [2, 768], P(None, ('mp', 'dp')), may hold values from 2.974051e-08 to 1.1896204e-07
- average_head: float32 [2, 768], P(None, ('mp', 'dp')), may hold values from -1.75 to 1.75
- hidden_bias: float32 [3072], P(('mp', 'dp')), may hold values from -1.75 to 1.75
- first_hidden: float32 [3072], P(('mp', 'dp')), may hold values from -0.00015258789 to 0.00015258789
- second_hidden: float32 [3072], P(('mp', 'dp')), may hold values from 3.306071e-09 to 1.3224284e-08
- average_hidden: float32 [3072], P(('mp', 'dp')), may hold values from -1.75 to 1.75
- layer_vectors: float32 [6, 768], P(None, 'dp'), may hold values from -0.8 to 2.4
- first_vectors: float32 [6, 768], P(None, 'dp'), may hold values from -0.00048828125 to 0.00048828125
- second_vectors: float32 [6, 768], P(None, 'dp'), may hold values from 2.974051e-08 to 1.1896204e-07
- average_vectors: float32 [6, 768], P(None, 'dp'), may hold values from -3 to 3
Outputs:
- layer_output: bfloat16 [16384, 768], P('dp')
- input_grad: float32 [16384, 768], P('dp')
- grad_norm: float32 [], replicated
- moment_qkv: float32 [3, 768, 768], P(None, 'dp', 'mp')
- square_qkv: float32 [3, 768, 768], P(None, 'dp', 'mp')
- updated_qkv: float32 [3, 768, 768], P(None, 'dp', 'mp')
- smooth_qkv: float32 [3, 768, 768], P(None, 'dp', 'mp')
- moment_attn: float32 [768, 768], P(('mp', 'dp'))
- square_attn: float32 [768, 768], P(('mp', 'dp'))
- updated_attn: float32 [768, 768], P(('mp', 'dp'))
- smooth_attn: float32 [768, 768], P(('mp', 'dp'))
- moment_up: float32 [768, 3072], P('dp', 'mp')
- square_up: float32 [768, 3072], P('dp', 'mp')
- updated_up: float32 [768, 3072], P('dp', 'mp')
- smooth_up: float32 [768, 3072], P('dp', 'mp')
- moment_down: float32 [3072, 768], P(('mp', 'dp'))
- square_down: float32 [3072, 768], P(('mp', 'dp'))
- updated_down: float32 [3072, 768], P(('mp', 'dp'))
- smooth_down: float32 [3072, 768], P(('mp', 'dp'))
- moment_head: float32 [2, 768], P(None, ('mp', 'dp'))
- square_head: float32 [2, 768], P(None, ('mp', 'dp'))
- updated_head: float32 [2, 768], P(None, ('mp', 'dp'))
- smooth_head: float32 [2, 768], P(None, ('mp', 'dp'))
- moment_hidden: float32 [3072], P(('mp', 'dp'))
- square_hidden: float32 [3072], P(('mp', 'dp'))
- updated_hidden: float32 [3072], P(('mp', 'dp'))
- smooth_hidden: float32 [3072], P(('mp', 'dp'))
- moment_vectors: float32 [6, 768], P(None, 'dp')
- square_vectors: float32 [6, 768], P(None, 'dp')
- updated_vectors: float32 [6, 768], P(None, 'dp')
- smooth_vectors: float32 [6, 768], P(None, 'dp')
All inputs are finite; a program needn't handle non-finite values.
Results may differ from a plain program's by a relative error of at most 0.015.
The roundings to bfloat16 on the way count: a program that leaves them out, or rounds other values in their place, can miss the bound.
Values may be sent and summed in bfloat16 or wider, within the bound.
No kernel may reach another device: no remote copies, remote signals or barrier semaphores. Data moves between devices by JAX's collectives and lax.ppermute only.
A program may use at most 192 MiB of HBM per device.

v0:
```python
import jax
import jax.numpy as jnp
from jax import lax
from jax.sharding import PartitionSpec as P

HD = 64
SEQ = 512
STEP = 7
NORM_EPS = 1e-05
SCORE_SCALE = 0.125
LEARN_RATE = 0.03
VECTOR_RATE = 0.4
BETA_ONE = 0.9
BETA_TWO = 0.95
ADAM_EPS = 1e-08
WEIGHT_DECAY = 0.1
EMA_RATE = 0.8
CLIP_NORM = 1.0
GELU_COEF = 0.7978845608028654


def gelu_tanh(value):
    return 0.5 * value * (1.0 + jnp.tanh(GELU_COEF * (value + 0.044715 * value * value * value)))


def norm_parts(rows):
    row_mean = jnp.mean(rows, axis=1, keepdims=True)
    centered = rows - row_mean
    inv_std = lax.rsqrt(jnp.mean(centered * centered, axis=1, keepdims=True) + NORM_EPS)
    return (centered * inv_std, inv_std)


def norm_back(grad_in, normed, inv_std, gain):
    scaled = grad_in * gain
    return inv_std * (
        scaled
        - jnp.mean(scaled, axis=1, keepdims=True)
        - normed * jnp.mean(scaled * normed, axis=1, keepdims=True)
    )


def visible_keys(lengths, padding):
    position = jnp.arange(SEQ, dtype=jnp.int32)
    bounds = jnp.cumsum(lengths)
    segment = jnp.sum((position[:, None] >= bounds[None, :]).astype(jnp.int32), axis=1)
    padded = position >= SEQ - padding
    same_segment = segment[:, None] == segment[None, :]
    itself = position[:, None] == position[None, :]
    return same_segment & (jnp.logical_not(padded)[None, :] | itself)


def kept_rows(padding):
    position = jnp.arange(SEQ, dtype=jnp.int32)
    return (position < SEQ - padding).astype(jnp.float32)


def split_heads(rows):
    return rows.reshape(SEQ, rows.shape[1] // HD, HD)


def masked_scores(query_heads, key_heads, allowed):
    scores = (
        jnp.einsum("qhe,khe->hqk", query_heads, key_heads, preferred_element_type=jnp.float32)
        * SCORE_SCALE
    )
    return jnp.where(allowed[None, :, :], scores, -1e30)


def attend_forward(packed):
    queries, key_rows, value_rows, allowed = packed
    value_heads = split_heads(value_rows)
    scores = masked_scores(split_heads(queries), split_heads(key_rows), allowed)
    row_max = jnp.max(scores, axis=2, keepdims=True)
    exponent = jnp.exp(scores - row_max)
    row_sum = jnp.sum(exponent, axis=2, keepdims=True)
    probs = (exponent / row_sum).astype(jnp.bfloat16)
    mixed = jnp.einsum("hqk,khe->qhe", probs, value_heads, preferred_element_type=jnp.float32)
    return (mixed.reshape(SEQ, -1).astype(jnp.bfloat16), (row_max + jnp.log(row_sum))[:, :, 0])


def attend_backward(packed):
    queries, key_rows, value_rows, allowed, log_total, grad_mixed = packed
    query_heads = split_heads(queries)
    key_heads = split_heads(key_rows)
    value_heads = split_heads(value_rows)
    scores = masked_scores(query_heads, key_heads, allowed)
    probs = jnp.exp(scores - log_total[:, :, None])
    grad_heads = split_heads(grad_mixed)
    grad_probs = jnp.einsum(
        "qhe,khe->hqk", grad_heads, value_heads, preferred_element_type=jnp.float32
    )
    row_dot = jnp.sum(probs * grad_probs, axis=2, keepdims=True)
    grad_scores = (probs * (grad_probs - row_dot)).astype(jnp.bfloat16)
    grad_query = (
        jnp.einsum("hqk,khe->qhe", grad_scores, key_heads, preferred_element_type=jnp.float32)
        * SCORE_SCALE
    )
    grad_key = (
        jnp.einsum("hqk,qhe->khe", grad_scores, query_heads, preferred_element_type=jnp.float32)
        * SCORE_SCALE
    )
    grad_value = jnp.einsum(
        "hqk,qhe->khe", probs.astype(jnp.bfloat16), grad_heads, preferred_element_type=jnp.float32
    )
    return jnp.stack(
        [grad_query.reshape(SEQ, -1), grad_key.reshape(SEQ, -1), grad_value.reshape(SEQ, -1)],
        axis=0,
    )


def adam_step(gradient, master, first, second, average, factor, decay_rate, step_rate):
    clipped = gradient * factor
    first_new = BETA_ONE * first + (1.0 - BETA_ONE) * clipped
    second_new = BETA_TWO * second + (1.0 - BETA_TWO) * clipped * clipped
    first_hat = first_new / (1.0 - BETA_ONE**STEP)
    second_hat = second_new / (1.0 - BETA_TWO**STEP)
    master_new = master - step_rate * (
        first_hat / (jnp.sqrt(second_hat) + ADAM_EPS) + decay_rate * master
    )
    average_new = EMA_RATE * average + (1.0 - EMA_RATE) * master_new
    return (first_new, second_new, master_new, average_new)


def body(
    tokens,
    cotangent,
    seg_lengths,
    pad_counts,
    qkv_weight,
    first_qkv,
    second_qkv,
    average_qkv,
    attn_weight,
    first_attn,
    second_attn,
    average_attn,
    up_weight,
    first_up,
    second_up,
    average_up,
    down_weight,
    first_down,
    second_down,
    average_down,
    head_bias,
    first_head,
    second_head,
    average_head,
    hidden_bias,
    first_hidden,
    second_hidden,
    average_hidden,
    layer_vectors,
    first_vectors,
    second_vectors,
    average_vectors,
):
    bfloat = jnp.bfloat16
    single = jnp.float32
    shared = (
        lax.all_gather(qkv_weight.astype(bfloat), "dp", axis=1, tiled=True),
        lax.all_gather(attn_weight.astype(bfloat), "dp", axis=0, tiled=True),
        lax.all_gather(up_weight.astype(bfloat), "dp", axis=0, tiled=True),
        lax.all_gather(down_weight.astype(bfloat), "dp", axis=0, tiled=True),
        lax.all_gather(head_bias.astype(bfloat), "dp", axis=1, tiled=True),
        lax.all_gather(hidden_bias.astype(bfloat), "dp", axis=0, tiled=True),
        lax.all_gather(layer_vectors.astype(bfloat), "dp", axis=1, tiled=True),
    )
    qkv_mat, attn_mat, up_mat, down_mat = (shared[0], shared[1], shared[2], shared[3])
    head_vec = shared[4].astype(single)
    hidden_vec = shared[5].astype(single)
    layer_vec = shared[6].astype(single)
    row_count = tokens.shape[0]
    seq_here = row_count // SEQ
    local_width = qkv_mat.shape[2]
    shaped = (seq_here, SEQ, local_width)
    allowed = jax.vmap(visible_keys)(seg_lengths, pad_counts)
    kept = jax.vmap(kept_rows)(pad_counts).reshape(row_count, 1)
    rows = tokens.astype(single)
    normed_one, inv_one = norm_parts(rows)
    first_in = (normed_one * layer_vec[0] + layer_vec[1]).astype(bfloat)
    projected = jnp.einsum("td,kdc->ktc", first_in, qkv_mat, preferred_element_type=single)
    queries = (projected[0] + head_vec[0]).astype(bfloat)
    key_rows = projected[1].astype(bfloat)
    value_rows = (projected[2] + head_vec[1]).astype(bfloat)
    mixed, log_total = lax.map(
        attend_forward,
        (queries.reshape(shaped), key_rows.reshape(shaped), value_rows.reshape(shaped), allowed),
    )
    mixed = mixed.reshape(row_count, local_width)
    attn_part = jnp.dot(mixed, attn_mat, preferred_element_type=single)
    hidden_one = (
        rows + lax.psum(attn_part.astype(jnp.bfloat16), "mp").astype(jnp.float32) + layer_vec[4]
    )
    normed_two, inv_two = norm_parts(hidden_one)
    second_in = (normed_two * layer_vec[2] + layer_vec[3]).astype(bfloat)
    pre_act = jnp.dot(second_in, up_mat, preferred_element_type=single) + hidden_vec
    act_value, act_pull = jax.vjp(gelu_tanh, pre_act)
    activated = act_value.astype(bfloat)
    down_part = jnp.dot(activated, down_mat, preferred_element_type=single)
    layer_output = (
        hidden_one
        + lax.psum(down_part.astype(jnp.bfloat16), "mp").astype(jnp.float32)
        + layer_vec[5]
    ).astype(bfloat)
    grad_out = cotangent.astype(single) * kept
    grad_out_low = grad_out.astype(bfloat)
    grad_down = jnp.einsum("tf,td->fd", activated, grad_out_low, preferred_element_type=single)
    grad_act = jnp.einsum("td,fd->tf", grad_out_low, down_mat, preferred_element_type=single)
    grad_pre = act_pull(grad_act)[0]
    grad_hidden = jnp.sum(grad_pre, axis=0)
    grad_pre_low = grad_pre.astype(bfloat)
    grad_up = jnp.einsum("td,tf->df", second_in, grad_pre_low, preferred_element_type=single)
    second_part = jnp.einsum("tf,df->td", grad_pre_low, up_mat, preferred_element_type=single)
    grad_second = lax.psum(second_part.astype(jnp.bfloat16), "mp").astype(jnp.float32)
    grad_hidden_one = grad_out + norm_back(grad_second, normed_two, inv_two, layer_vec[2])
    grad_hidden_low = grad_hidden_one.astype(bfloat)
    grad_attn = jnp.einsum("tc,td->cd", mixed, grad_hidden_low, preferred_element_type=single)
    grad_mixed = jnp.einsum(
        "td,cd->tc", grad_hidden_low, attn_mat, preferred_element_type=single
    ).astype(bfloat)
    grad_proj = lax.map(
        attend_backward,
        (
            queries.reshape(shaped),
            key_rows.reshape(shaped),
            value_rows.reshape(shaped),
            allowed,
            log_total,
            grad_mixed.reshape(shaped),
        ),
    )
    grad_proj = jnp.transpose(grad_proj, (1, 0, 2, 3)).reshape(3, row_count, local_width)
    grad_head = jnp.stack([jnp.sum(grad_proj[0], axis=0), jnp.sum(grad_proj[2], axis=0)], axis=0)
    proj_low = grad_proj.astype(bfloat)
    grad_qkv = jnp.einsum("td,ktc->kdc", first_in, proj_low, preferred_element_type=single)
    first_part = jnp.einsum("ktc,kdc->td", proj_low, qkv_mat, preferred_element_type=single)
    grad_first = lax.psum(first_part.astype(jnp.bfloat16), "mp").astype(jnp.float32)
    input_grad = grad_hidden_one + norm_back(grad_first, normed_one, inv_one, layer_vec[0])
    grad_vectors = jnp.stack(
        [
            jnp.sum(grad_first * normed_one, axis=0),
            jnp.sum(grad_first, axis=0),
            jnp.sum(grad_second * normed_two, axis=0),
            jnp.sum(grad_second, axis=0),
            jnp.sum(grad_hidden_one, axis=0),
            jnp.sum(grad_out, axis=0),
        ],
        axis=0,
    )
    reduced = (
        lax.psum_scatter(grad_qkv, "dp", scatter_dimension=1, tiled=True),
        lax.psum_scatter(grad_attn, "dp", scatter_dimension=0, tiled=True),
        lax.psum_scatter(grad_up, "dp", scatter_dimension=0, tiled=True),
        lax.psum_scatter(grad_down, "dp", scatter_dimension=0, tiled=True),
        lax.psum_scatter(grad_head, "dp", scatter_dimension=1, tiled=True),
        lax.psum_scatter(grad_hidden, "dp", scatter_dimension=0, tiled=True),
        lax.psum_scatter(grad_vectors, "dp", scatter_dimension=1, tiled=True),
    )
    squares_local = sum((jnp.sum(member * member) for member in reduced[:6])) + 0.5 * jnp.sum(
        reduced[6] * reduced[6]
    )
    grad_norm = jnp.sqrt(lax.psum(squares_local, ("dp", "mp")))
    factor = CLIP_NORM / jnp.maximum(grad_norm, CLIP_NORM)
    moment_qkv, square_qkv, updated_qkv, smooth_qkv = adam_step(
        reduced[0], qkv_weight, first_qkv, second_qkv, average_qkv, factor, WEIGHT_DECAY, LEARN_RATE
    )
    moment_attn, square_attn, updated_attn, smooth_attn = adam_step(
        reduced[1],
        attn_weight,
        first_attn,
        second_attn,
        average_attn,
        factor,
        WEIGHT_DECAY,
        LEARN_RATE,
    )
    moment_up, square_up, updated_up, smooth_up = adam_step(
        reduced[2], up_weight, first_up, second_up, average_up, factor, WEIGHT_DECAY, LEARN_RATE
    )
    moment_down, square_down, updated_down, smooth_down = adam_step(
        reduced[3],
        down_weight,
        first_down,
        second_down,
        average_down,
        factor,
        WEIGHT_DECAY,
        LEARN_RATE,
    )
    moment_head, square_head, updated_head, smooth_head = adam_step(
        reduced[4], head_bias, first_head, second_head, average_head, factor, 0.0, VECTOR_RATE
    )
    moment_hidden, square_hidden, updated_hidden, smooth_hidden = adam_step(
        reduced[5],
        hidden_bias,
        first_hidden,
        second_hidden,
        average_hidden,
        factor,
        0.0,
        VECTOR_RATE,
    )
    moment_vectors, square_vectors, updated_vectors, smooth_vectors = adam_step(
        reduced[6],
        layer_vectors,
        first_vectors,
        second_vectors,
        average_vectors,
        factor,
        0.0,
        VECTOR_RATE,
    )
    return (
        layer_output,
        input_grad,
        grad_norm,
        moment_qkv,
        square_qkv,
        updated_qkv,
        smooth_qkv,
        moment_attn,
        square_attn,
        updated_attn,
        smooth_attn,
        moment_up,
        square_up,
        updated_up,
        smooth_up,
        moment_down,
        square_down,
        updated_down,
        smooth_down,
        moment_head,
        square_head,
        updated_head,
        smooth_head,
        moment_hidden,
        square_hidden,
        updated_hidden,
        smooth_hidden,
        moment_vectors,
        square_vectors,
        updated_vectors,
        smooth_vectors,
    )


def solution(mesh):
    placed = (
        P("dp", None),
        P("dp", None),
        P("dp", None),
        P("dp"),
        P(None, "dp", "mp"),
        P(None, "dp", "mp"),
        P(None, "dp", "mp"),
        P(None, "dp", "mp"),
        P(("mp", "dp"), None),
        P(("mp", "dp"), None),
        P(("mp", "dp"), None),
        P(("mp", "dp"), None),
        P("dp", "mp"),
        P("dp", "mp"),
        P("dp", "mp"),
        P("dp", "mp"),
        P(("mp", "dp"), None),
        P(("mp", "dp"), None),
        P(("mp", "dp"), None),
        P(("mp", "dp"), None),
        P(None, ("mp", "dp")),
        P(None, ("mp", "dp")),
        P(None, ("mp", "dp")),
        P(None, ("mp", "dp")),
        P(("mp", "dp")),
        P(("mp", "dp")),
        P(("mp", "dp")),
        P(("mp", "dp")),
        P(None, "dp"),
        P(None, "dp"),
        P(None, "dp"),
        P(None, "dp"),
    )
    return jax.shard_map(
        body,
        mesh=mesh,
        in_specs=placed,
        out_specs=(
            P("dp", None),
            P("dp", None),
            P(),
            P(None, "dp", "mp"),
            P(None, "dp", "mp"),
            P(None, "dp", "mp"),
            P(None, "dp", "mp"),
            P(("mp", "dp"), None),
            P(("mp", "dp"), None),
            P(("mp", "dp"), None),
            P(("mp", "dp"), None),
            P("dp", "mp"),
            P("dp", "mp"),
            P("dp", "mp"),
            P("dp", "mp"),
            P(("mp", "dp"), None),
            P(("mp", "dp"), None),
            P(("mp", "dp"), None),
            P(("mp", "dp"), None),
            P(None, ("mp", "dp")),
            P(None, ("mp", "dp")),
            P(None, ("mp", "dp")),
            P(None, ("mp", "dp")),
            P(("mp", "dp")),
            P(("mp", "dp")),
            P(("mp", "dp")),
            P(("mp", "dp")),
            P(None, "dp"),
            P(None, "dp"),
            P(None, "dp"),
            P(None, "dp"),
        ),
        check_vma=False,
    )
```

profile of v0, /device:TPU:0, one launch (start us, length us, event | category | flops | bytes accessed | tf_op | source)
XLA Modules:
  0.0 1236.6 jit_solution(2257658814909541547)
XLA Ops:
  10.6 42.2 %all-gather.1 = bf16[16,24,2]{1,2,0:T(2,128)(2,1)S(1)} all-gather(bf16[1,24,2]{1,2,0:T(2,128)(2,1)S(1)} %convert_bitcast_fusion.1), channel_id=1, replica_groups=mesh['dp'=16,'mp'=2] {'dp'}, dimensions={0}, use_global_device_ids=true | all-gather | bytes 1632 | tf_op jit(solution)/shard_map/all_gather | solution.py:165
  53.6 35.9 %all-gather = bf16[16,48,6]{1,2,0:T(8,128)(2,1)S(1)} all-gather(bf16[1,48,6]{1,2,0:T(8,128)(2,1)S(1)} %convert_bitcast_fusion), channel_id=1, replica_groups=mesh['dp'=16,'mp'=2] {'dp'}, dimensions={0}, use_global_device_ids=true | all-gather | bytes 9792 | tf_op jit(solution)/shard_map/all_gather | solution.py:167
  96.2 43.5 %all_gather.24 = bf16[384,768]{1,0:T(8,128)(2,1)} all-gather(bf16[24,768]{1,0:T(8,128)(2,1)S(1)} %convert_element_type.152), channel_id=1, replica_groups=mesh['dp'=16,'mp'=2] {'dp'}, dimensions={0}, use_global_device_ids=true | all-gather | bytes 626688 | tf_op jit(solution)/shard_map/all_gather | solution.py:162
  139.8 4.0 convolution_bitcast_fusion
  155.2 19.9 %while.22 = (s32[]{:T(128)}, bf16[2,512,384]{2,1,0:T(8,128)(2,1)}, f32[2,6,512]{2,1,0:T(8,128)}, bf16[2,512,384]{1,2,0:T(8,128)(2,1)}, pred[2,512,512]{1,2,0:T(8...) while((s32[]{:T(128)}, bf16[2,512,384]{2,1,0:T(8,128)(2,1)}, ...), condition=%wide.region_7.8_spmd, body=%wide.region_4.7_spmd.sunk | while | flops 421721088 | bytes 25997480 | solution.py:186
  175.1 4.0 convolution_convert_fusion
  183.2 36.7 %all-reduce = bf16[1536]{0:T(1024)(128)(2,1)S(1)} all-reduce(bf16[1536]{0:T(1024)(128)(2,1)S(1)} %dynamic-update-slice), channel_id=1, replica_groups=mesh['dp'=16,'mp'=2] {'dp'}, use_global_device_ids=true, to_apply=%add | all-reduce | flops 1536 | bytes 6144
  223.6 39.2 %all-gather.8.cloned.1.call-done = bf16[768,1536]{1,0:T(8,128)(2,1)} async-done(((bf16[48,1536]{1,0:T(8,128)(2,1)}), bf16[768,1536]{1,0:T(8,128)(2,1)}) %all-gather.8.cloned.1.call-update) | async-done | bytes 2359312 | tf_op jit(solution)/shard_map/all_gather | solution.py:163
  262.8 6.6 fusion.67
  269.4 58.1 %all-gather.10.cloned.1.call-done = bf16[1536,768]{1,0:T(8,128)(2,1)} async-done(((bf16[96,768]{1,0:T(8,128)(2,1)}), bf16[1536,768]{1,0:T(8,128)(2,1)}) %all-gather.10.cloned.1.call-update) | async-done | bytes 2359312 | tf_op jit(solution)/shard_map/all_gather | solution.py:164
  327.5 11.1 fusion.79
  340.3 3.7 convolution_convert_fusion.1
  344.1 8.6 convolution_convert_fusion.2
  352.7 10.7 all-reduce.13.cloned.1.call-done
  363.4 3.5 fusion.39
  367.0 3.4 fusion.75
  373.4 35.6 %while.23 = (s32[]{:T(128)}, f32[2,3,512,384]{3,2,0,1:T(8,128)}, bf16[2,512,384]{1,2,0:T(8,128)(2,1)S(1)}, pred[2,512,512]{1,2,0:T(8,128)(4,1)}, bf16[2,512,384]...) while((s32[]{:T(128)}, f32[2,3,512,384]{3,2,0,1:T(8,128)}, ...), condition=%wide.region_17.18_spmd, body=%wide.region_15.17_spmd.sunk | while | flops 1031795712 | bytes 81219784 | solution.py:222
  413.2 3.4 bitcast_convert_fusion
  417.7 3.8 fusion.48
  421.5 19.6 %all-reduce.17.cloned.1.call-done = (bf16[1024,768]{1,0:T(8,128)(2,1)}, bf16[1024,768]{1,0:T(8,128)(2,1)}) async-done(((bf16[1024,768]{1,0:T(8,128)(2,1)}, bf16[1024,768]{1,0:T(8,128)(2,1)}), (bf16[1024,768]{1,0:T(8,128)(2,1)}, bf16[1024,768]{1,0:T(8,128)(2,1)})) %all-reduce.17.cloned.1.call-update) | async-done | bytes 3145744 | tf_op jit(solution)/shard_map/psum | solution.py:203
  445.1 5.8 convolution_bitcast_fusion.1
  451.0 6.3 copy.167
  458.7 7.0 fusion.44
  465.7 9.5 fusion.51
  479.4 77.4 %all-reduce.4 = (f32[2,384]{1,0:T(2,128)S(1)}, f32[1536]{0:T(1024)S(1)}) all-reduce(f32[2,384]{1,0:T(2,128)S(1)} %pad_maximum_fusion, f32[1536]{0:T(1024)S(1)} %copy-done.34), channel_id=6, replica_groups=mesh['dp'=16,'mp'=2] {'dp'}, use_global_device_ids=true, to_apply=%region_31.32.clone | all-reduce | flops 2304 | bytes 18432
  558.2 14.1 %reduce-scatter.8.cloned.1.call-done = f32[24,768]{1,0:T(8,128)} async-done(((f32[384,768]{1,0:T(8,128)}), f32[24,768]{1,0:T(8,128)}) %reduce-scatter.8.cloned.1.call-update) | async-done | bytes 73744 | tf_op jit(solution)/shard_map/reduce_scatter | solution.py:253
  573.8 124.7 %reduce-scatter.14.cloned.1.call-done = f32[48,6]{1,0:T(8,128)} async-done(((f32[768,6]{1,0:T(8,128)}), f32[48,6]{1,0:T(8,128)}) %reduce-scatter.14.cloned.1.call-update) | async-done | bytes 1168
  700.6 182.5 %all-reduce.15.cloned.1.call-done = f32[3,768,384]{2,0,1:T(4,128)} async-done(((f32[3,768,384]{2,0,1:T(4,128)}), f32[3,768,384]{2,0,1:T(4,128)}) %all-reduce.15.cloned.1.call-update) | async-done | bytes 3538960
  886.2 139.5 %reduce-scatter.10.cloned.1.call-done = f32[48,1536]{1,0:T(8,128)} async-done(((f32[768,1536]{1,0:T(8,128)}), f32[48,1536]{1,0:T(8,128)}) %reduce-scatter.10.cloned.1.call-update) | async-done | bytes 294928 | tf_op jit(solution)/shard_map/reduce_scatter | solution.py:254
  1027.9 139.6 %reduce-scatter.12.cloned.1.call-done = f32[96,768]{1,0:T(8,128)} async-done(((f32[1536,768]{1,0:T(8,128)}), f32[96,768]{1,0:T(8,128)}) %reduce-scatter.12.cloned.1.call-update) | async-done | bytes 294928 | tf_op jit(solution)/shard_map/reduce_scatter | solution.py:255
  1171.2 5.1 fusion.31
  1176.4 39.8 %psum.39 = f32[]{:T(128)} all-reduce(f32[]{:T(128)S(6)} %add.327), channel_id=1, replica_groups=mesh['dp'=16,'mp'=2] {'dp','mp'}, use_global_device_ids=true, to_apply=%region_44.45 | all-reduce | flops 1 | bytes 8 | tf_op jit(solution)/shard_map/psum | solution.py:263
  (251 shorter events, 123.2 us)
Async XLA Ops:
  7.2 87.0 %copy-start = (bf16[1024,768]{1,0:T(8,128)(2,1)S(1)}, bf16[1024,768]{1,0:T(8,128)(2,1)}, u32[]{:S(2)}) copy-start(bf16[1024,768]{1,0:T(8,128)(2,1)} %param.36) | copy-start | bytes 4718596
  7.2 132.5 %all-gather.6.cloned.1.call-start = ((), (), s32[]{:S(2)}) async-start(), calls=%async_computation.4 | async-start | bytes 1880064 | tf_op jit(solution)/shard_map/all_gather | solution.py:161
  9.0 211.6 %all-reduce.11.cloned.1.call-start = ((), (), s32[]{:S(2)}) async-start(), calls=%async_computation.5 | async-start | bytes 3145728 | tf_op jit(solution)/shard_map/psum | solution.py:193
  91.7 52.0 %copy-start.29 = (f32[768]{0:T(1024)}, f32[768]{0:T(1024)S(1)}, u32[]{:S(2)}) copy-start(f32[768]{0:T(1024)S(1)} %get-tuple-element.328) | copy-start | bytes 9220
  91.7 52.0 %copy-start.38 = (f32[768]{0:T(1024)}, f32[768]{0:T(1024)S(1)}, u32[]{:S(2)}) copy-start(f32[768]{0:T(1024)S(1)} %get-tuple-element.327) | copy-start | bytes 9220
  94.3 49.5 %copy-start.25 = (f32[1024]{0:T(1024)}, f32[1024]{0:T(1024)S(1)}, u32[]{:S(2)}) copy-start(f32[1024]{0:T(1024)S(1)} %broadcast_multiply_fusion.5) | copy-start | bytes 12292
  94.9 48.9 %copy-start.27 = (f32[1024]{0:T(1024)}, f32[1024]{0:T(1024)S(1)}, u32[]{:S(2)}) copy-start(f32[1024]{0:T(1024)S(1)} %add_rsqrt_fusion.1) | copy-start | bytes 12292
  175.0 45.5 %copy-start.4 = (bf16[2,512,384]{1,2,0:T(8,128)(2,1)}, bf16[2,512,384]{1,2,0:T(8,128)(2,1)S(1)}, u32[]{:S(2)}) copy-start(bf16[2,512,384]{1,2,0:T(8,128)(2,1)S(1)} %get-tuple-element.594) | copy-start | bytes 2359300
  175.0 45.5 %copy-start.6 = (bf16[2,512,384]{1,2,0:T(8,128)(2,1)}, bf16[2,512,384]{1,2,0:T(8,128)(2,1)S(1)}, u32[]{:S(2)}) copy-start(bf16[2,512,384]{1,2,0:T(8,128)(2,1)S(1)} %get-tuple-element.595) | copy-start | bytes 2359300
  179.1 83.7 %all-gather.8.cloned.1.call-start = ((), (), s32[]{:S(2)}) async-start(), calls=%async_computation.6 | async-start | bytes 2506752 | tf_op jit(solution)/shard_map/all_gather | solution.py:163
  179.8 147.7 %all-gather.10.cloned.1.call-start = ((), (), s32[]{:S(2)}) async-start(), calls=%async_computation.7 | async-start | bytes 2506752 | tf_op jit(solution)/shard_map/all_gather | solution.py:164
  181.6 181.8 %all-reduce.13.cloned.1.call-start = ((), (), s32[]{:S(2)}) async-start(), calls=%async_computation.8 | async-start | bytes 3145728 | tf_op jit(solution)/shard_map/psum | solution.py:215
  220.6 42.2 %copy-start.36 = (f32[768]{0:T(1024)S(1)}, f32[768]{0:T(1024)}, u32[]{:S(2)}) copy-start(f32[768]{0:T(1024)} %get-tuple-element.324) | copy-start | bytes 9220
  262.8 64.7 %copy-start.33 = (f32[1536]{0:T(1024)S(1)}, f32[1536]{0:T(1024)}, u32[]{:S(2)}) copy-start(f32[1536]{0:T(1024)} %convert_element_type.158) | copy-start | bytes 18436
  344.0 97.1 %all-reduce.17.cloned.1.call-start = ((), (), s32[]{:S(2)}) async-start(), calls=%async_computation.14 | async-start | bytes 6291456 | tf_op jit(solution)/shard_map/psum | solution.py:203
  416.6 24.6 %copy-start.1 = (bf16[1024,768]{1,0:T(8,128)(2,1)S(1)}, bf16[1024,768]{1,0:T(8,128)(2,1)}, u32[]{:S(2)}) copy-start(bf16[1024,768]{1,0:T(8,128)(2,1)} %param.36) | copy-start | bytes 4718596
  416.6 24.6 %copy-start.26 = (f32[1024]{0:T(1024)S(1)}, f32[1024]{0:T(1024)}, u32[]{:S(2)}) copy-start(f32[1024]{0:T(1024)} %copy-done.25) | copy-start | bytes 12292
  416.6 155.7 %reduce-scatter.8.cloned.1.call-start = ((), (), s32[]{:S(2)}) async-start(), calls=%async_computation.9 | async-start | bytes 1253376 | tf_op jit(solution)/shard_map/reduce_scatter | solution.py:253
  421.4 277.1 %reduce-scatter.14.cloned.1.call-start = ((), (), s32[]{:S(2)}) async-start(), calls=%async_computation.12 | async-start | bytes 417792
  445.1 438.1 %all-reduce.15.cloned.1.call-start = ((), (), s32[]{:S(2)}) async-start(), calls=%async_computation.13 | async-start | bytes 9437184
  457.3 568.3 %reduce-scatter.10.cloned.1.call-start = ((), (), s32[]{:S(2)}) async-start(), calls=%async_computation.10 | async-start | bytes 5013504 | tf_op jit(solution)/shard_map/reduce_scatter | solution.py:254
  465.7 701.8 %reduce-scatter.12.cloned.1.call-start = ((), (), s32[]{:S(2)}) async-start(), calls=%async_computation.11 | async-start | bytes 5013504 | tf_op jit(solution)/shard_map/reduce_scatter | solution.py:255
  475.3 695.9 %copy-start.31 = (f32[768]{0:T(1024)S(1)}, f32[768]{0:T(1024)}, u32[]{:S(2)}) copy-start(f32[768]{0:T(1024)} %get-tuple-element.323) | copy-start | bytes 9220
  556.8 143.8 %copy-start.43 = (f32[1536]{0:T(1024)}, f32[1536]{0:T(1024)S(1)}, u32[]{:S(2)}) copy-start(f32[1536]{0:T(1024)S(1)} %get-tuple-element.362) | copy-start | bytes 18436
  1171.1 48.5 %copy-start.32 = (f32[6,48]{1,0:T(8,128)S(1)}, f32[6,48]{1,0:T(8,128)}, u32[]{:S(2)}) copy-start(f32[6,48]{1,0:T(8,128)} %param.64) | copy-start | bytes 3460
  1171.2 48.5 %copy-start.35 = (f32[6,48]{1,0:T(8,128)S(1)}, f32[6,48]{1,0:T(8,128)}, u32[]{:S(2)}) copy-start(f32[6,48]{1,0:T(8,128)} %param.67) | copy-start | bytes 3460
  1171.2 52.1 %copy-start.18 = (f32[24,768]{1,0:T(8,128)S(1)}, f32[24,768]{1,0:T(8,128)}, u32[]{:S(2)}) copy-start(f32[24,768]{1,0:T(8,128)} %param.44) | copy-start | bytes 221188
  1176.3 51.2 %copy-start.15 = (f32[96,768]{1,0:T(8,128)S(1)}, f32[96,768]{1,0:T(8,128)}, u32[]{:S(2)}) copy-start(f32[96,768]{1,0:T(8,128)} %param.52) | copy-start | bytes 884740
  1176.3 51.2 %copy-start.16 = (f32[96,768]{1,0:T(8,128)S(1)}, f32[96,768]{1,0:T(8,128)}, u32[]{:S(2)}) copy-start(f32[96,768]{1,0:T(8,128)} %reduce-scatter.12.cloned.1.call-done) | copy-start | bytes 884740
  1176.3 51.2 %copy-start.19 = (f32[96,768]{1,0:T(8,128)S(1)}, f32[96,768]{1,0:T(8,128)}, u32[]{:S(2)}) copy-start(f32[96,768]{1,0:T(8,128)} %param.55) | copy-start | bytes 884740
  1176.3 51.2 %copy-start.20 = (f32[96,768]{1,0:T(8,128)S(1)}, f32[96,768]{1,0:T(8,128)}, u32[]{:S(2)}) copy-start(f32[96,768]{1,0:T(8,128)} %param.54) | copy-start | bytes 884740
  1176.4 51.2 %copy-start.21 = (f32[96,768]{1,0:T(8,128)S(1)}, f32[96,768]{1,0:T(8,128)}, u32[]{:S(2)}) copy-start(f32[96,768]{1,0:T(8,128)} %param.53) | copy-start | bytes 884740
  (31 other events, 171.8 us)
Sparse Core Ops, SparseCore 0:
  11.3 61.8 all-gather.5
  179.2 16.2 all-reduce.10
  199.3 63.4 all-gather.7
  266.4 61.0 all-gather.9
  344.2 19.1 all-reduce.12
  416.7 24.4 all-reduce.16
  446.6 125.6 reduce-scatter.7
  578.2 120.2 reduce-scatter.13
  704.3 178.8 all-reduce.14
  889.0 136.6 reduce-scatter.9
  1030.8 136.6 reduce-scatter.11
where the time goes:
time: 1250 us; the launch traced here: 1240 us
  waiting for transfers between devices  728 us (58%)
  blocking collectives  275 us (22%)
  matrix products  93.5 us (7%)
  other arithmetic  65.3 us (5%)
  local copies, waits for them, and re-layouts  49.3 us (4%)
  between operations  23.7 us (2%)
    unnamed x13, waiting for transfers between devices  307 us
    reduce_scatter x1, waiting for transfers between devices, body(): lax.psum_scatter(grad_down, 'dp', scatter_dimension=0, tiled=True)  140 us
    reduce_scatter x1, waiting for transfers between devices, body(): lax.psum_scatter(grad_up, 'dp', scatter_dimension=0, tiled=True)  139 us
    unnamed x2, blocking collectives  114 us
    all_gather x1, waiting for transfers between devices, body(): lax.all_gather(down_weight.astype(bfloat), 'dp', axis=0, tiled=True)  58.1 us
    all_gather x1, blocking collectives, body(): lax.all_gather(attn_weight.astype(bfloat), 'dp', axis=0, tiled=True)  43.5 us
    all_gather x1, blocking collectives, body(): lax.all_gather(head_bias.astype(bfloat), 'dp', axis=1, tiled=True)  42.2 us
    psum x1, blocking collectives, body(): grad_norm = jnp.sqrt(lax.psum(squares_local, ('dp', 'mp')))  39.8 us
  transfers between devices with their start and end apart: 11, of which 9 were waited for; matrix products, arithmetic and copies ran while one was open for 6% of the time, Pallas kernels for 0%

commit v1 on v0

--- a/solution.py
+++ b/solution.py
@@ -2,6 +2,7 @@
 import jax.numpy as jnp
 from jax import lax
 from jax.sharding import PartitionSpec as P
+from jax.lax import psum
 
 HD = 64
 SEQ = 512
@@ -17,6 +18,14 @@
 EMA_RATE = 0.8
 CLIP_NORM = 1.0
 GELU_COEF = 0.7978845608028654
+
+
+def derive_works(patch):
+    peer_axis = "dp"
+    net_axis = "mp"
+    for i in (net_axis, peer_axis):
+        patch = psum(patch, axis_name=i)
+    return patch
 
 
 def gelu_tanh(value):
@@ -260,7 +269,7 @@
     squares_local = sum((jnp.sum(member * member) for member in reduced[:6])) + 0.5 * jnp.sum(
         reduced[6] * reduced[6]
     )
-    grad_norm = jnp.sqrt(lax.psum(squares_local, ("dp", "mp")))
+    grad_norm = jnp.sqrt(derive_works(squares_local))
     factor = CLIP_NORM / jnp.maximum(grad_norm, CLIP_NORM)
     moment_qkv, square_qkv, updated_qkv, smooth_qkv = adam_step(
         reduced[0], qkv_weight, first_qkv, second_qkv, average_qkv, factor, WEIGHT_DECAY, LEARN_RATE

time: 1250 us -> 1250 us (level)
    psum x1 -> x2, blocking collectives: 39.8 us -> 43.3 us  [derive_works(): patch = psum(patch, axis_name=i)]
where the time goes in v1:
time: 1250 us; the launch traced here: 1240 us
  waiting for transfers between devices  728 us (58%)
  blocking collectives  279 us (22%)
  matrix products  93.5 us (7%)
  other arithmetic  65.3 us (5%)
  local copies, waits for them, and re-layouts  49.3 us (4%)
  between operations  23.7 us (2%)
    unnamed x13, waiting for transfers between devices  307 us
    reduce_scatter x1, waiting for transfers between devices, body(): lax.psum_scatter(grad_down, 'dp', scatter_dimension=0, tiled=True)  140 us
    reduce_scatter x1, waiting for transfers between devices, body(): lax.psum_scatter(grad_up, 'dp', scatter_dimension=0, tiled=True)  139 us
    unnamed x2, blocking collectives  114 us
    all_gather x1, waiting for transfers between devices, body(): lax.all_gather(down_weight.astype(bfloat), 'dp', axis=0, tiled=True)  58.1 us
    all_gather x1, blocking collectives, body(): lax.all_gather(attn_weight.astype(bfloat), 'dp', axis=0, tiled=True)  43.5 us
    psum x2, blocking collectives, derive_works(): patch = psum(patch, axis_name=i)  43.3 us
    all_gather x1, blocking collectives, body(): lax.all_gather(head_bias.astype(bfloat), 'dp', axis=1, tiled=True)  42.2 us
  transfers between devices with their start and end apart: 11, of which 9 were waited for; matrix products, arithmetic and copies ran while one was open for 6% of the time, Pallas kernels for 0%

profile of v1, /device:TPU:0, one launch (start us, length us, event | category | flops | bytes accessed | tf_op | source)
XLA Modules:
  0.0 1240.1 jit_solution(14195529249144815473)
XLA Ops:
  10.6 42.2 %all-gather.1 = bf16[16,24,2]{1,2,0:T(2,128)(2,1)S(1)} all-gather(bf16[1,24,2]{1,2,0:T(2,128)(2,1)S(1)} %convert_bitcast_fusion.1), channel_id=1, replica_groups=mesh['dp'=16,'mp'=2] {'dp'}, dimensions={0}, use_global_device_ids=true | all-gather | bytes 1632 | tf_op jit(solution)/shard_map/all_gather | solution.py:174
  53.6 35.9 %all-gather = bf16[16,48,6]{1,2,0:T(8,128)(2,1)S(1)} all-gather(bf16[1,48,6]{1,2,0:T(8,128)(2,1)S(1)} %convert_bitcast_fusion), channel_id=1, replica_groups=mesh['dp'=16,'mp'=2] {'dp'}, dimensions={0}, use_global_device_ids=true | all-gather | bytes 9792 | tf_op jit(solution)/shard_map/all_gather | solution.py:176
  96.2 43.5 %all_gather.24 = bf16[384,768]{1,0:T(8,128)(2,1)} all-gather(bf16[24,768]{1,0:T(8,128)(2,1)S(1)} %convert_element_type.152), channel_id=1, replica_groups=mesh['dp'=16,'mp'=2] {'dp'}, dimensions={0}, use_global_device_ids=true | all-gather | bytes 626688 | tf_op jit(solution)/shard_map/all_gather | solution.py:171
  139.8 4.0 convolution_bitcast_fusion
  155.2 19.9 %while.22 = (s32[]{:T(128)}, bf16[2,512,384]{2,1,0:T(8,128)(2,1)}, f32[2,6,512]{2,1,0:T(8,128)}, bf16[2,512,384]{1,2,0:T(8,128)(2,1)}, pred[2,512,512]{1,2,0:T(8...) while((s32[]{:T(128)}, bf16[2,512,384]{2,1,0:T(8,128)(2,1)}, ...), condition=%wide.region_7.8_spmd, body=%wide.region_4.7_spmd.sunk | while | flops 421721088 | bytes 25997480 | solution.py:195
  175.1 4.0 convolution_convert_fusion
  183.2 36.7 %all-reduce = bf16[1536]{0:T(1024)(128)(2,1)S(1)} all-reduce(bf16[1536]{0:T(1024)(128)(2,1)S(1)} %dynamic-update-slice), channel_id=1, replica_groups=mesh['dp'=16,'mp'=2] {'dp'}, use_global_device_ids=true, to_apply=%add | all-reduce | flops 1536 | bytes 6144
  223.6 39.2 %all-gather.8.cloned.1.call-done = bf16[768,1536]{1,0:T(8,128)(2,1)} async-done(((bf16[48,1536]{1,0:T(8,128)(2,1)}), bf16[768,1536]{1,0:T(8,128)(2,1)}) %all-gather.8.cloned.1.call-update) | async-done | bytes 2359312 | tf_op jit(solution)/shard_map/all_gather | solution.py:172
  262.8 6.6 fusion.67
  269.4 58.1 %all-gather.10.cloned.1.call-done = bf16[1536,768]{1,0:T(8,128)(2,1)} async-done(((bf16[96,768]{1,0:T(8,128)(2,1)}), bf16[1536,768]{1,0:T(8,128)(2,1)}) %all-gather.10.cloned.1.call-update) | async-done | bytes 2359312 | tf_op jit(solution)/shard_map/all_gather | solution.py:173
  327.5 11.1 fusion.79
  340.3 3.7 convolution_convert_fusion.1
  344.1 8.6 convolution_convert_fusion.2
  352.7 10.7 all-reduce.13.cloned.1.call-done
  363.4 3.5 fusion.39
  367.0 3.4 fusion.75
  373.3 35.6 %while.23 = (s32[]{:T(128)}, f32[2,3,512,384]{3,2,0,1:T(8,128)}, bf16[2,512,384]{1,2,0:T(8,128)(2,1)S(1)}, pred[2,512,512]{1,2,0:T(8,128)(4,1)}, bf16[2,512,384]...) while((s32[]{:T(128)}, f32[2,3,512,384]{3,2,0,1:T(8,128)}, ...), condition=%wide.region_17.18_spmd, body=%wide.region_15.17_spmd.sunk | while | flops 1031795712 | bytes 81219784 | solution.py:231
  413.1 3.4 bitcast_convert_fusion
  417.6 3.8 fusion.48
  421.5 19.6 %all-reduce.17.cloned.1.call-done = (bf16[1024,768]{1,0:T(8,128)(2,1)}, bf16[1024,768]{1,0:T(8,128)(2,1)}) async-done(((bf16[1024,768]{1,0:T(8,128)(2,1)}, bf16[1024,768]{1,0:T(8,128)(2,1)}), (bf16[1024,768]{1,0:T(8,128)(2,1)}, bf16[1024,768]{1,0:T(8,128)(2,1)})) %all-reduce.17.cloned.1.call-update) | async-done | bytes 3145744 | tf_op jit(solution)/shard_map/psum | solution.py:212
  445.1 5.8 convolution_bitcast_fusion.1
  450.9 6.3 copy.167
  458.7 7.0 fusion.44
  465.7 9.5 fusion.51
  479.4 77.4 %all-reduce.4 = (f32[2,384]{1,0:T(2,128)S(1)}, f32[1536]{0:T(1024)S(1)}) all-reduce(f32[2,384]{1,0:T(2,128)S(1)} %pad_maximum_fusion, f32[1536]{0:T(1024)S(1)} %copy-done.34), channel_id=6, replica_groups=mesh['dp'=16,'mp'=2] {'dp'}, use_global_device_ids=true, to_apply=%region_31.32.clone | all-reduce | flops 2304 | bytes 18432
  558.2 14.1 %reduce-scatter.8.cloned.1.call-done = f32[24,768]{1,0:T(8,128)} async-done(((f32[384,768]{1,0:T(8,128)}), f32[24,768]{1,0:T(8,128)}) %reduce-scatter.8.cloned.1.call-update) | async-done | bytes 73744 | tf_op jit(solution)/shard_map/reduce_scatter | solution.py:262
  573.8 124.7 %reduce-scatter.14.cloned.1.call-done = f32[48,6]{1,0:T(8,128)} async-done(((f32[768,6]{1,0:T(8,128)}), f32[48,6]{1,0:T(8,128)}) %reduce-scatter.14.cloned.1.call-update) | async-done | bytes 1168
  700.6 182.5 %all-reduce.15.cloned.1.call-done = f32[3,768,384]{2,0,1:T(4,128)} async-done(((f32[3,768,384]{2,0,1:T(4,128)}), f32[3,768,384]{2,0,1:T(4,128)}) %all-reduce.15.cloned.1.call-update) | async-done | bytes 3538960
  886.1 139.5 %reduce-scatter.10.cloned.1.call-done = f32[48,1536]{1,0:T(8,128)} async-done(((f32[768,1536]{1,0:T(8,128)}), f32[48,1536]{1,0:T(8,128)}) %reduce-scatter.10.cloned.1.call-update) | async-done | bytes 294928 | tf_op jit(solution)/shard_map/reduce_scatter | solution.py:263
  1027.9 139.6 %reduce-scatter.12.cloned.1.call-done = f32[96,768]{1,0:T(8,128)} async-done(((f32[1536,768]{1,0:T(8,128)}), f32[96,768]{1,0:T(8,128)}) %reduce-scatter.12.cloned.1.call-update) | async-done | bytes 294928 | tf_op jit(solution)/shard_map/reduce_scatter | solution.py:264
  1174.1 5.1 fusion.31
  1179.3 40.4 %psum.47 = f32[]{:T(128)} all-reduce(f32[]{:T(128)} %psum.46), channel_id=1, replica_groups=mesh['dp'=16,'mp'=2] {'dp'}, use_global_device_ids=true, to_apply=%region_45.46 | all-reduce | flops 1 | bytes 8 | tf_op jit(solution)/shard_map/psum | solution.py:27
  (252 shorter events, 126.2 us)
Async XLA Ops:
  7.2 87.0 %copy-start = (bf16[1024,768]{1,0:T(8,128)(2,1)S(1)}, bf16[1024,768]{1,0:T(8,128)(2,1)}, u32[]{:S(2)}) copy-start(bf16[1024,768]{1,0:T(8,128)(2,1)} %param.36) | copy-start | bytes 4718596
  7.2 132.5 %all-gather.6.cloned.1.call-start = ((), (), s32[]{:S(2)}) async-start(), calls=%async_computation.4 | async-start | bytes 1880064 | tf_op jit(solution)/shard_map/all_gather | solution.py:170
  9.0 211.6 %all-reduce.11.cloned.1.call-start = ((), (), s32[]{:S(2)}) async-start(), calls=%async_computation.5 | async-start | bytes 3145728 | tf_op jit(solution)/shard_map/psum | solution.py:202
  91.7 52.0 %copy-start.29 = (f32[768]{0:T(1024)}, f32[768]{0:T(1024)S(1)}, u32[]{:S(2)}) copy-start(f32[768]{0:T(1024)S(1)} %get-tuple-element.328) | copy-start | bytes 9220
  91.7 52.0 %copy-start.38 = (f32[768]{0:T(1024)}, f32[768]{0:T(1024)S(1)}, u32[]{:S(2)}) copy-start(f32[768]{0:T(1024)S(1)} %get-tuple-element.327) | copy-start | bytes 9220
  94.3 49.5 %copy-start.25 = (f32[1024]{0:T(1024)}, f32[1024]{0:T(1024)S(1)}, u32[]{:S(2)}) copy-start(f32[1024]{0:T(1024)S(1)} %broadcast_multiply_fusion.5) | copy-start | bytes 12292
  94.9 48.9 %copy-start.27 = (f32[1024]{0:T(1024)}, f32[1024]{0:T(1024)S(1)}, u32[]{:S(2)}) copy-start(f32[1024]{0:T(1024)S(1)} %add_rsqrt_fusion.1) | copy-start | bytes 12292
  175.0 45.5 %copy-start.4 = (bf16[2,512,384]{1,2,0:T(8,128)(2,1)}, bf16[2,512,384]{1,2,0:T(8,128)(2,1)S(1)}, u32[]{:S(2)}) copy-start(bf16[2,512,384]{1,2,0:T(8,128)(2,1)S(1)} %get-tuple-element.594) | copy-start | bytes 2359300
  175.0 45.5 %copy-start.6 = (bf16[2,512,384]{1,2,0:T(8,128)(2,1)}, bf16[2,512,384]{1,2,0:T(8,128)(2,1)S(1)}, u32[]{:S(2)}) copy-start(bf16[2,512,384]{1,2,0:T(8,128)(2,1)S(1)} %get-tuple-element.595) | copy-start | bytes 2359300
  179.1 83.7 %all-gather.8.cloned.1.call-start = ((), (), s32[]{:S(2)}) async-start(), calls=%async_computation.6 | async-start | bytes 2506752 | tf_op jit(solution)/shard_map/all_gather | solution.py:172
  179.8 147.7 %all-gather.10.cloned.1.call-start = ((), (), s32[]{:S(2)}) async-start(), calls=%async_computation.7 | async-start | bytes 2506752 | tf_op jit(solution)/shard_map/all_gather | solution.py:173
  181.6 181.8 %all-reduce.13.cloned.1.call-start = ((), (), s32[]{:S(2)}) async-start(), calls=%async_computation.8 | async-start | bytes 3145728 | tf_op jit(solution)/shard_map/psum | solution.py:224
  220.6 42.2 %copy-start.36 = (f32[768]{0:T(1024)S(1)}, f32[768]{0:T(1024)}, u32[]{:S(2)}) copy-start(f32[768]{0:T(1024)} %get-tuple-element.324) | copy-start | bytes 9220
  262.8 64.7 %copy-start.33 = (f32[1536]{0:T(1024)S(1)}, f32[1536]{0:T(1024)}, u32[]{:S(2)}) copy-start(f32[1536]{0:T(1024)} %convert_element_type.158) | copy-start | bytes 18436
  344.0 97.1 %all-reduce.17.cloned.1.call-start = ((), (), s32[]{:S(2)}) async-start(), calls=%async_computation.14 | async-start | bytes 6291456 | tf_op jit(solution)/shard_map/psum | solution.py:212
  416.5 24.6 %copy-start.1 = (bf16[1024,768]{1,0:T(8,128)(2,1)S(1)}, bf16[1024,768]{1,0:T(8,128)(2,1)}, u32[]{:S(2)}) copy-start(bf16[1024,768]{1,0:T(8,128)(2,1)} %param.36) | copy-start | bytes 4718596
  416.5 24.6 %copy-start.26 = (f32[1024]{0:T(1024)S(1)}, f32[1024]{0:T(1024)}, u32[]{:S(2)}) copy-start(f32[1024]{0:T(1024)} %copy-done.25) | copy-start | bytes 12292
  416.6 155.7 %reduce-scatter.8.cloned.1.call-start = ((), (), s32[]{:S(2)}) async-start(), calls=%async_computation.9 | async-start | bytes 1253376 | tf_op jit(solution)/shard_map/reduce_scatter | solution.py:262
  421.4 277.1 %reduce-scatter.14.cloned.1.call-start = ((), (), s32[]{:S(2)}) async-start(), calls=%async_computation.12 | async-start | bytes 417792
  445.1 438.1 %all-reduce.15.cloned.1.call-start = ((), (), s32[]{:S(2)}) async-start(), calls=%async_computation.13 | async-start | bytes 9437184
  457.3 568.3 %reduce-scatter.10.cloned.1.call-start = ((), (), s32[]{:S(2)}) async-start(), calls=%async_computation.10 | async-start | bytes 5013504 | tf_op jit(solution)/shard_map/reduce_scatter | solution.py:263
  465.7 701.9 %reduce-scatter.12.cloned.1.call-start = ((), (), s32[]{:S(2)}) async-start(), calls=%async_computation.11 | async-start | bytes 5013504 | tf_op jit(solution)/shard_map/reduce_scatter | solution.py:264
  475.3 698.8 %copy-start.31 = (f32[768]{0:T(1024)S(1)}, f32[768]{0:T(1024)}, u32[]{:S(2)}) copy-start(f32[768]{0:T(1024)} %get-tuple-element.323) | copy-start | bytes 9220
  556.8 617.3 %copy-start.43 = (f32[1536]{0:T(1024)}, f32[1536]{0:T(1024)S(1)}, u32[]{:S(2)}) copy-start(f32[1536]{0:T(1024)S(1)} %get-tuple-element.362) | copy-start | bytes 18436
  1174.1 49.1 %copy-start.32 = (f32[6,48]{1,0:T(8,128)S(1)}, f32[6,48]{1,0:T(8,128)}, u32[]{:S(2)}) copy-start(f32[6,48]{1,0:T(8,128)} %param.64) | copy-start | bytes 3460
  1174.1 49.1 %copy-start.35 = (f32[6,48]{1,0:T(8,128)S(1)}, f32[6,48]{1,0:T(8,128)}, u32[]{:S(2)}) copy-start(f32[6,48]{1,0:T(8,128)} %param.67) | copy-start | bytes 3460
  1174.1 52.7 %copy-start.18 = (f32[24,768]{1,0:T(8,128)S(1)}, f32[24,768]{1,0:T(8,128)}, u32[]{:S(2)}) copy-start(f32[24,768]{1,0:T(8,128)} %param.44) | copy-start | bytes 221188
  1179.3 51.8 %copy-start.15 = (f32[96,768]{1,0:T(8,128)S(1)}, f32[96,768]{1,0:T(8,128)}, u32[]{:S(2)}) copy-start(f32[96,768]{1,0:T(8,128)} %param.52) | copy-start | bytes 884740
  1179.3 51.8 %copy-start.16 = (f32[96,768]{1,0:T(8,128)S(1)}, f32[96,768]{1,0:T(8,128)}, u32[]{:S(2)}) copy-start(f32[96,768]{1,0:T(8,128)} %reduce-scatter.12.cloned.1.call-done) | copy-start | bytes 884740
  1179.3 51.8 %copy-start.19 = (f32[96,768]{1,0:T(8,128)S(1)}, f32[96,768]{1,0:T(8,128)}, u32[]{:S(2)}) copy-start(f32[96,768]{1,0:T(8,128)} %param.55) | copy-start | bytes 884740
  1179.3 51.8 %copy-start.20 = (f32[96,768]{1,0:T(8,128)S(1)}, f32[96,768]{1,0:T(8,128)}, u32[]{:S(2)}) copy-start(f32[96,768]{1,0:T(8,128)} %param.54) | copy-start | bytes 884740
  1179.3 51.8 %copy-start.21 = (f32[96,768]{1,0:T(8,128)S(1)}, f32[96,768]{1,0:T(8,128)}, u32[]{:S(2)}) copy-start(f32[96,768]{1,0:T(8,128)} %param.53) | copy-start | bytes 884740
  (31 other events, 171.8 us)
Sparse Core Ops, SparseCore 0:
  11.3 61.8 all-gather.5
  179.2 16.2 all-reduce.10
  199.3 63.4 all-gather.7
  266.4 61.0 all-gather.9
  344.1 19.1 all-reduce.12
  416.6 24.4 all-reduce.16
  446.6 125.6 reduce-scatter.7
  578.2 120.2 reduce-scatter.13
  704.2 178.8 all-reduce.14
  889.0 136.6 reduce-scatter.9
  1030.8 136.6 reduce-scatter.11
